TPU v7x, 32 devices: a whole 2x2x4 slice. The times are simulated.
32 devices in a mesh: dp: 4 (over x, core), expert: 8 (over z, y).
Axes of the slice: x: 2, y: 2, z: 4, core: 2. Of those that a mesh axis runs over, the one named last changes fastest.
Arguments:
- tokens: bfloat16 [4096, 2048], P(('dp', 'expert')), may hold values from -6 to 6
- expert_ids: int32 [4096, 8], P(('dp', 'expert')), may hold values from 0 to 127, all different within a row; in each aligned block of 128 rows (0 to 127, 128 to 255, ...) at most 20 rows name the same one
- gate_probs: float32 [4096, 8], P(('dp', 'expert')), may hold values from 0.05 to 1
- gate_weight: bfloat16 [128, 768, 2048], P(('dp', 'expert')), may hold values from -0.125 to 0.125
- up_weight: bfloat16 [128, 768, 2048], P(('dp', 'expert')), may hold values from -0.125 to 0.125
- down_weight: bfloat16 [128, 768, 2048], P(('dp', 'expert')), may hold values from -0.4375 to 0.4375
Outputs:
- mixed: bfloat16 [4096, 2048], P(('dp', 'expert'))
- expert_load: float32 [128], replicated
Inputs may be any that keep to these rules, and one draw needn't show every extreme that they name: `expert_ids`: in each block of 128 consecutive tokens no expert is named by more than 20 pairs, a bound that some blocks reach; every expert is named somewhere.
All inputs are finite; a program needn't handle non-finite values.
Results may differ from a plain program's by a relative error of at most 0.0085.
Values may be sent and summed in bfloat16 or wider, within the bound.
A program may use at most 128 MiB of HBM per device.

v0:
```python
import jax
import jax.numpy as jnp
from jax import lax
from jax.sharding import PartitionSpec as P

CAP = 20


def expert_block(arrived, gate_weight, up_weight, down_weight):
    gate_part = jnp.einsum(
        "sekd,efd->sekf", arrived, gate_weight, preferred_element_type=jnp.float32
    )
    up_part = jnp.einsum("sekd,efd->sekf", arrived, up_weight, preferred_element_type=jnp.float32)
    hidden = (jax.nn.silu(gate_part) * up_part).astype(jnp.bfloat16)
    produced = jnp.einsum("sekf,efd->sekd", hidden, down_weight, preferred_element_type=jnp.float32)
    return produced.astype(jnp.bfloat16)


def on_device(tokens, expert_ids, gate_probs, gate_weight, up_weight, down_weight):
    tok_rows, features = tokens.shape
    chosen = expert_ids.shape[1]
    owned = gate_weight.shape[0]
    devices = lax.axis_size(("dp", "expert"))
    experts = owned * devices
    pairs = tok_rows * chosen
    flat_ids = expert_ids.reshape(pairs)
    one_hot = (flat_ids[:, None] == lax.iota(jnp.int32, experts)[None, :]).astype(jnp.int32)
    earlier = jnp.cumsum(one_hot, axis=0) - one_hot
    slot_index = jnp.sum(earlier * one_hot, axis=1)
    target = flat_ids * CAP + slot_index
    owner_row = lax.iota(jnp.int32, pairs) // chosen
    source_row = jnp.full((experts * CAP,), tok_rows, jnp.int32).at[target].set(owner_row)
    padded = jnp.concatenate([tokens, jnp.zeros((1, features), tokens.dtype)], axis=0)
    outgoing = padded[source_row].reshape(devices, owned, CAP, features)
    counts = lax.psum(jnp.sum(one_hot, axis=0).astype(jnp.float32), ("dp", "expert"))
    produced = expert_block(
        lax.all_to_all(outgoing, ("dp", "expert"), split_axis=0, concat_axis=0, tiled=True),
        gate_weight,
        up_weight,
        down_weight,
    )
    returned = lax.all_to_all(produced, ("dp", "expert"), split_axis=0, concat_axis=0, tiled=True)
    results = returned.reshape(experts * CAP, features)
    picked = results[target].reshape(tok_rows, chosen, features)
    weights = gate_probs / jnp.sum(gate_probs, axis=1, keepdims=True)
    mixed = jnp.einsum("tk,tkd->td", weights, picked.astype(jnp.float32)).astype(jnp.bfloat16)
    expert_load = counts * (experts / (tok_rows * devices * chosen))
    return (mixed, expert_load)


def solution(mesh):
    in_specs = (
        P(("dp", "expert"), None),
        P(("dp", "expert"), None),
        P(("dp", "expert"), None),
        P(("dp", "expert"), None, None),
        P(("dp", "expert"), None, None),
        P(("dp", "expert"), None, None),
    )
    out_specs = (P(("dp", "expert"), None), P())
    return jax.shard_map(
        on_device, mesh=mesh, in_specs=in_specs, out_specs=out_specs, check_vma=False
    )
```

profile of v0, /device:TPU:0, one launch (start us, length us, event | category | flops | bytes accessed | tf_op | source)
XLA Modules:
  0.0 692.8 jit_solution(644135197542510640)
XLA Ops:
  0.6 0.8 copy.24
  1.6 0.7 broadcast_multiply_fusion
  2.4 0.2 fusion.22
  2.7 0.1 copy.27
  3.0 0.4 convert_reduce_fusion
  3.4 4.3 scatter_custom_fusion
  7.7 1.1 concatenate.3
  8.8 10.9 %gather_fusion = bf16[2560,2048]{1,0:T(8,128)(2,1)} fusion(bf16[129,2048]{1,0:T(8,128)(2,1)S(1)} %concatenate.3, s32[3072]{0:T(1024)S(1)} %pad_clamp_fusion), kind=kCustom, calls=%fused_computation | custom fusion | bytes 20981760 | tf_op jit(solution)/shard_map/gather | solution.py:34
  19.7 16.4 %reshape.61 = bf16[32,4,20,2048]{3,2,1,0:T(8,128)(2,1)} reshape(bf16[2560,2048]{1,0:T(8,128)(2,1)} %gather_fusion) | data formatting | bytes 20971520 | tf_op jit(solution)/shard_map/reshape | solution.py:34
  36.1 12.8 %copy.28 = bf16[32,4,20,2048]{3,1,2,0:T(4,128)(2,1)S(1)} copy(bf16[32,4,20,2048]{3,2,1,0:T(8,128)(2,1)} %reshape.61) | data formatting | bytes 20971520 | tf_op jit(solution)/shard_map/reshape | solution.py:34
  48.9 237.2 %all_to_all.10 = bf16[32,4,20,2048]{3,1,2,0:T(4,128)(2,1)} all-to-all(bf16[32,4,20,2048]{3,1,2,0:T(4,128)(2,1)S(1)} %copy.28), channel_id=1, replica_groups=mesh['dp'=4,'expert'=8] {'dp','expert'}, dimensions={0} | all-to-all | bytes 20971520 | tf_op jit(solution)/shard_map/all_to_all | solution.py:37
  286.1 27.1 %fusion.2 = f32[4,32,20,768]{3,1,2,0:T(8,128)} fusion(bf16[4,768,2048]{2,1,0:T(8,128)(2,1)} %param.10, bf16[32,4,20,2048]{3,1,2,0:T(4,128)(2,1)} %all_to_all.10), kind=kOutput, calls=%fused_computation.5 | convolution fusion | flops 8053063680 | bytes 30932992 | tf_op jit(solution)/shard_map/sekd,efd->sekf/dot_general | solution.py:13
  313.2 32.7 %fusion.8 = bf16[32,4,20,768]{3,0,2,1:T(8,128)(2,1)} fusion(f32[4,32,20,768]{3,1,2,0:T(8,128)} %fusion.2, bf16[4,768,2048]{2,1,0:T(8,128)(2,1)} %param.9, bf16[32,4,20,2048]{3,1,2,0:T(4,128)(2,1)} %all_to_all.10), kind=kOutput, calls=%fused_computation.13 | convolution fusion | flops 8064860160 | bytes 34865152 | tf_op jit(solution)/shard_map/sekd,efd->sekf/dot_general | solution.py:10
  345.9 14.2 %convert_bitcast_fusion = bf16[32,4,20,2048]{3,0,2,1:T(8,128)(2,1)S(1)} fusion(bf16[32,4,20,768]{3,0,2,1:T(8,128)(2,1)} %fusion.8, bf16[4,768,2048]{2,1,0:T(8,128)(2,1)} %param.11), kind=kOutput, calls=%fused_computation.9 | convolution fusion | flops 8058306560 | bytes 27000832 | tf_op jit(solution)/shard_map/sekf,efd->sekd/dot_general | solution.py:15
  360.2 24.1 %copy.31 = bf16[32,4,20,2048]{3,1,2,0:T(4,128)(2,1)} copy(bf16[32,4,20,2048]{3,0,2,1:T(8,128)(2,1)S(1)} %convert_bitcast_fusion) | data formatting | bytes 20971520 | tf_op jit(solution)/shard_map/convert_element_type | solution.py:16
  384.3 3.9 all-to-all-start.1
  388.2 0.1 copy.36
  388.3 254.7 %psum.7 = f32[128]{0:T(128)S(1)} all-reduce(f32[128]{0:T(128)S(1)} %convert_element_type.29), channel_id=1, replica_groups=mesh['dp'=4,'expert'=8] {'dp','expert'}, use_global_device_ids=true, to_apply=%region_6.7 | all-reduce | flops 128 | bytes 1024 | tf_op jit(solution)/shard_map/psum | solution.py:35
  643.0 0.5 broadcast_multiply_fusion.1
  643.5 14.0 %copy.32 = bf16[32,4,20,2048]{3,2,1,0:T(8,128)(2,1)} copy(bf16[32,4,20,2048]{3,1,2,0:T(4,128)(2,1)} %all-to-all-done.1) | data formatting | bytes 20971520 | tf_op jit(solution)/shard_map/all_to_all | solution.py:42
  657.5 16.5 %reshape.62 = bf16[2560,2048]{1,0:T(8,128)(2,1)} reshape(bf16[32,4,20,2048]{3,2,1,0:T(8,128)(2,1)} %copy.32) | data formatting | bytes 20971520 | tf_op jit(solution)/shard_map/reshape | solution.py:43
  674.0 14.2 %gather_fusion.1 = bf16[1024,2048]{1,0:T(8,128)(2,1)} fusion(bf16[2560,2048]{1,0:T(8,128)(2,1)} %reshape.62, s32[1024]{0:T(1024)S(1)} %broadcast_clamp_fusion), kind=kCustom, calls=%fused_computation.1 | custom fusion | bytes 8392704 | tf_op jit(solution)/shard_map/gather | solution.py:44
  688.1 3.4 fusion.18
  691.6 1.1 copy.45
  (20 shorter events, 0.6 us)
Async XLA Ops:
  384.3 3.9 copy-start
  384.3 259.3 %all-to-all-start.1 = ((bf16[32,4,20,2048]{3,1,2,0:T(4,128)(2,1)}), bf16[32,4,20,2048]{3,1,2,0:T(4,128)(2,1)}, u32[]{:S(2)}, u32[]{:S(2)}) async-start(bf16[32,4,20,2048]{3,1,2,0:T(4,128)(2,1)} %copy.31), calls=%async_computation.1 | async-start | bytes 20971520 | tf_op jit(solution)/shard_map/all_to_all | solution.py:42
where the time goes:
time: 698 us; the launch traced here: 693 us
  blocking collectives  492 us (70%)
  local copies, waits for them, and re-layouts  117 us (17%)
  matrix products  77.5 us (11%)
    psum x1, blocking collectives, on_device(): lax.psum(jnp.sum(one_hot, axis=0).astype(jnp.float32), ('dp', 'expert'))  255 us
    all_to_all x1, blocking collectives, on_device(): lax.all_to_all(outgoing, ('dp', 'expert'), split_axis=0, concat_axis=0, t...  237 us
    dot_general x1, matrix products, expert_block(): jnp.einsum('sekd,efd->sekf', arrived, gate_weight, preferred_element_type...  32.7 us
    reshape x2, local copies, waits for them, and re-layouts, on_device(): outgoing = padded[source_row].reshape(devices, owned, CAP, features)  29.1 us
    dot_general x1, matrix products, expert_block(): jnp.einsum('sekd,efd->sekf', arrived, up_weight, preferred_element_type=j...  27.1 us
    convert_element_type x1, local copies, waits for them, and re-layouts, expert_block(): return produced.astype(jnp.bfloat16)  24.1 us
    reshape x1, local copies, waits for them, and re-layouts, on_device(): results = returned.reshape(experts * CAP, features)  16.5 us
    dot_general x1, matrix products, expert_block(): jnp.einsum('sekf,efd->sekd', hidden, down_weight, preferred_element_type=...  14.2 us
  transfers between devices with their start and end apart: 1, of which 0 were waited for; matrix products, arithmetic and copies ran while one was open for 0% of the time, Pallas kernels for 0%

commit v1 on v0

--- a/solution.py
+++ b/solution.py
@@ -32,7 +32,9 @@
     source_row = jnp.full((experts * CAP,), tok_rows, jnp.int32).at[target].set(owner_row)
     padded = jnp.concatenate([tokens, jnp.zeros((1, features), tokens.dtype)], axis=0)
     outgoing = padded[source_row].reshape(devices, owned, CAP, features)
-    counts = lax.psum(jnp.sum(one_hot, axis=0).astype(jnp.float32), ("dp", "expert"))
+    counts = jnp.sum(
+        lax.all_gather(jnp.sum(one_hot, axis=0).astype(jnp.float32), ("dp", "expert")), axis=0
+    )
     produced = expert_block(
         lax.all_to_all(outgoing, ("dp", "expert"), split_axis=0, concat_axis=0, tiled=True),
         gate_weight,

time: 698 us -> 723 us (1.036)
  blocking collectives: 492 us -> 521 us
    all_gather x0 -> x1, blocking collectives: none -> 284 us  [on_device(): lax.all_gather(jnp.sum(one_hot, axis=0).astype(jnp.float32), ('dp', 'expe...]
    psum x1 -> x0, blocking collectives: 255 us -> none  [on_device(): lax.psum(jnp.sum(one_hot, axis=0).astype(jnp.float32), ('dp', 'expert'))]
where the time goes in v1:
time: 723 us; the launch traced here: 721 us
  blocking collectives  521 us (72%)
  local copies, waits for them, and re-layouts  117 us (16%)
  matrix products  76.7 us (11%)
    all_gather x1, blocking collectives, on_device(): lax.all_gather(jnp.sum(one_hot, axis=0).astype(jnp.float32), ('dp', 'expe...  284 us
    all_to_all x1, blocking collectives, on_device(): lax.all_to_all(outgoing, ('dp', 'expert'), split_axis=0, concat_axis=0, t...  237 us
    dot_general x1, matrix products, expert_block(): jnp.einsum('sekd,efd->sekf', arrived, gate_weight, preferred_element_type...  32.5 us
    reshape x2, local copies, waits for them, and re-layouts, on_device(): outgoing = padded[source_row].reshape(devices, owned, CAP, features)  29.1 us
    dot_general x1, matrix products, expert_block(): jnp.einsum('sekd,efd->sekf', arrived, up_weight, preferred_element_type=j...  27.1 us
    convert_element_type x1, local copies, waits for them, and re-layouts, expert_block(): return produced.astype(jnp.bfloat16)  24.1 us
    reshape x1, local copies, waits for them, and re-layouts, on_device(): results = returned.reshape(experts * CAP, features)  16.5 us
  transfers between devices with their start and end apart: 1, of which 0 were waited for; matrix products, arithmetic and copies ran while one was open for 0% of the time, Pallas kernels for 0%

profile of v1, /device:TPU:0, one launch (start us, length us, event | category | flops | bytes accessed | tf_op | source)
XLA Modules:
  0.0 721.3 jit_solution(1897470006476194372)
XLA Ops:
  0.6 0.8 copy.24
  1.6 0.7 broadcast_multiply_fusion
  2.4 0.2 fusion.22
  2.7 0.1 copy.27
  3.0 0.4 convert_reduce_fusion
  3.4 4.3 scatter_custom_fusion
  7.7 1.1 concatenate.3
  8.8 10.9 %gather_fusion = bf16[2560,2048]{1,0:T(8,128)(2,1)} fusion(bf16[129,2048]{1,0:T(8,128)(2,1)S(1)} %concatenate.3, s32[3072]{0:T(1024)S(1)} %pad_clamp_fusion), kind=kCustom, calls=%fused_computation | custom fusion | bytes 20981760 | tf_op jit(solution)/shard_map/gather | solution.py:34
  19.7 16.4 %reshape.69 = bf16[32,4,20,2048]{3,2,1,0:T(8,128)(2,1)} reshape(bf16[2560,2048]{1,0:T(8,128)(2,1)} %gather_fusion) | data formatting | bytes 20971520 | tf_op jit(solution)/shard_map/reshape | solution.py:34
  36.1 12.8 %copy.28 = bf16[32,4,20,2048]{3,1,2,0:T(4,128)(2,1)S(1)} copy(bf16[32,4,20,2048]{3,2,1,0:T(8,128)(2,1)} %reshape.69) | data formatting | bytes 20971520 | tf_op jit(solution)/shard_map/reshape | solution.py:34
  48.9 237.0 %all_to_all.10 = bf16[32,4,20,2048]{3,1,2,0:T(4,128)(2,1)} all-to-all(bf16[32,4,20,2048]{3,1,2,0:T(4,128)(2,1)S(1)} %copy.28), channel_id=1, replica_groups=mesh['dp'=4,'expert'=8] {'dp','expert'}, dimensions={0} | all-to-all | bytes 20971520 | tf_op jit(solution)/shard_map/all_to_all | solution.py:39
  285.8 27.1 %fusion.2 = f32[4,32,20,768]{3,1,2,0:T(8,128)} fusion(bf16[4,768,2048]{2,1,0:T(8,128)(2,1)} %param.10, bf16[32,4,20,2048]{3,1,2,0:T(4,128)(2,1)} %all_to_all.10), kind=kOutput, calls=%fused_computation.5 | convolution fusion | flops 8053063680 | bytes 30932992 | tf_op jit(solution)/shard_map/sekd,efd->sekf/dot_general | solution.py:13
  313.0 32.5 %fusion.8 = bf16[32,4,20,768]{3,0,2,1:T(8,128)(2,1)} fusion(f32[4,32,20,768]{3,1,2,0:T(8,128)} %fusion.2, bf16[4,768,2048]{2,1,0:T(8,128)(2,1)} %param.9, bf16[32,4,20,2048]{3,1,2,0:T(4,128)(2,1)} %all_to_all.10), kind=kOutput, calls=%fused_computation.13 | convolution fusion | flops 8064860160 | bytes 34865152 | tf_op jit(solution)/shard_map/sekd,efd->sekf/dot_general | solution.py:10
  345.4 13.7 %convert_bitcast_fusion = bf16[32,4,20,2048]{3,0,2,1:T(8,128)(2,1)S(1)} fusion(bf16[32,4,20,768]{3,0,2,1:T(8,128)(2,1)} %fusion.8, bf16[4,768,2048]{2,1,0:T(8,128)(2,1)} %param.11), kind=kOutput, calls=%fused_computation.9 | convolution fusion | flops 8058306560 | bytes 27000832 | tf_op jit(solution)/shard_map/sekf,efd->sekd/dot_general | solution.py:15
  359.1 24.1 %copy.31 = bf16[32,4,20,2048]{3,1,2,0:T(4,128)(2,1)} copy(bf16[32,4,20,2048]{3,0,2,1:T(8,128)(2,1)S(1)} %convert_bitcast_fusion) | data formatting | bytes 20971520 | tf_op jit(solution)/shard_map/convert_element_type | solution.py:16
  383.2 3.9 all-to-all-start.1
  387.1 0.1 copy.36
  387.3 284.0 %all-gather.1 = f32[32,1,128]{2,1,0:T(1,128)S(1)} all-gather(f32[1,1,128]{2,1,0:T(1,128)S(1)} %convert_bitcast_fusion.1), channel_id=2, replica_groups=mesh['dp'=4,'expert'=8] {'dp','expert'}, dimensions={0}, use_global_device_ids=true | all-gather | bytes 16896 | tf_op jit(solution)/shard_map/all_gather | solution.py:36
  671.4 0.5 broadcast_multiply_fusion.1
  671.9 14.3 %copy.32 = bf16[32,4,20,2048]{3,2,1,0:T(8,128)(2,1)} copy(bf16[32,4,20,2048]{3,1,2,0:T(4,128)(2,1)} %all-to-all-done.1) | data formatting | bytes 20971520 | tf_op jit(solution)/shard_map/all_to_all | solution.py:44
  686.2 16.5 %reshape.70 = bf16[2560,2048]{1,0:T(8,128)(2,1)} reshape(bf16[32,4,20,2048]{3,2,1,0:T(8,128)(2,1)} %copy.32) | data formatting | bytes 20971520 | tf_op jit(solution)/shard_map/reshape | solution.py:45
  702.7 14.2 %gather_fusion.1 = bf16[1024,2048]{1,0:T(8,128)(2,1)} fusion(bf16[2560,2048]{1,0:T(8,128)(2,1)} %reshape.70, s32[1024]{0:T(1024)S(1)} %broadcast_clamp_fusion), kind=kCustom, calls=%fused_computation.1 | custom fusion | bytes 8392704 | tf_op jit(solution)/shard_map/gather | solution.py:46
  716.8 3.4 fusion.18
  720.3 1.1 copy.45
  (21 shorter events, 0.7 us)
Async XLA Ops:
  383.2 3.9 copy-start
  383.2 288.7 %all-to-all-start.1 = ((bf16[32,4,20,2048]{3,1,2,0:T(4,128)(2,1)}), bf16[32,4,20,2048]{3,1,2,0:T(4,128)(2,1)}, u32[]{:S(2)}, u32[]{:S(2)}) async-start(bf16[32,4,20,2048]{3,1,2,0:T(4,128)(2,1)} %copy.31), calls=%async_computation.1 | async-start | bytes 20971520 | tf_op jit(solution)/shard_map/all_to_all | solution.py:44
